TPU v7x, 32 devices: a whole 2x2x4 slice. The times are simulated.
32 devices in a mesh: groups: 2 (over y), samp: 4 (over z), feat: 4 (over x, core).
Axes of the slice: x: 2, y: 2, z: 4, core: 2. Of those that a mesh axis runs over, the one named last changes fastest.
Arguments:
- x_blocks: bfloat16 [64, 64, 128, 128], P(('groups', 'samp'), 'feat'), parts along dimension 0, may hold values from -6 to 6
- block_cols: int32 [64, 64], P('groups', 'feat'), parts along dimension 0, may hold values from 0 to 31
- labels: int32 [8192], P('groups'), parts along dimension 0, may hold values from 0 to 63
- group_ids: int32 [8192], P('groups'), parts along dimension 0, may hold values from 0 to 7, as said below
- picks: int32 [3, 32], P(None, 'groups'), parts along dimension 1, may hold values from 0 to 31, as said below
- w_init: float32 [16384, 64], P('feat'), may hold values from -2.253903 to 2.253903
Outputs:
- scores: float32 [8192, 64], P(('groups', 'samp')), parts along dimension 0
- adversary: float32 [16], P('groups'), parts along dimension 0
There are 2 independent parts, one for each index of `groups`. A program takes and returns all parts, laid end to end along the dimension named above; an argument that names none is the same for every part. Nothing has to cross between parts.
Inputs may be any that keep to these rules, and one draw needn't show every extreme that they name: `group_ids`: every row block of 128 samples holds every group at least once. `picks`: the entries of one step are distinct. Row block b is owned by index b // 8 of samp. The k-th aligned block of 4 entries of a step is the list of index k of samp; it names row blocks owned by index k or by the next index along samp (index 0 after the last); between one and 2 entries of each list name the next index's row blocks, exactly 2 in at least one list of every step.
All inputs are finite; a program needn't handle non-finite values.
Results may differ from a plain program's by a relative error of at most 0.00315.
The roundings to bfloat16 on the way count: a program that leaves them out, or rounds other values in their place, can miss the bound.
Values may be sent and summed in bfloat16 or wider, within the bound.
No kernel may reach another device: no remote copies, remote signals or barrier semaphores. Data moves between devices by JAX's collectives and lax.ppermute only.
A program may use at most 64 MiB of HBM per device.

v0:
```python
import jax
import jax.numpy as jnp
from jax import lax
from jax.sharding import PartitionSpec as P

GRP = 8
STEPS = 3
weight_rate = 8.0
adv_rate = 2.0


def per_device(x_blocks, block_cols, labels, group_ids, picks, w_init):
    row_blocks, per_row, block_size, _ = x_blocks.shape
    feat_rows, classes = w_init.shape
    col_blocks = feat_rows // block_size
    total_blocks = block_cols.shape[0]
    feat_count = lax.axis_size("feat")
    my_index = lax.axis_index("samp")
    step_rate = weight_rate * picks.shape[1] / (per_row * feat_count)
    class_range = jnp.arange(classes, dtype=jnp.int32)
    group_range = jnp.arange(GRP, dtype=jnp.int32)
    block_range = jnp.arange(total_blocks, dtype=jnp.int32)
    col_range = jnp.arange(col_blocks, dtype=jnp.int32)
    sample_groups = (group_ids[:, None] == group_range[None, :]).astype(jnp.float32)
    block_groups = jnp.sum(sample_groups.reshape(total_blocks, block_size, GRP), axis=1)
    own_start = my_index * row_blocks
    own_cols = lax.dynamic_slice_in_dim(block_cols, own_start, row_blocks, 0)
    own_labels = lax.dynamic_slice_in_dim(
        labels, own_start * block_size, row_blocks * block_size, 0
    )
    own_groups = lax.dynamic_slice_in_dim(
        group_ids, own_start * block_size, row_blocks * block_size, 0
    )

    def total_logits(x_rows, col_rows, weights_bf):
        tiles = weights_bf.reshape(col_blocks, block_size, classes)[col_rows]
        partial_sum = jnp.einsum(
            "rbij,rbjc->ric", x_rows, tiles, preferred_element_type=jnp.float32
        )
        summed = lax.psum(partial_sum, "feat")
        return summed.reshape(-1, classes)

    def evaluate(row_data, weights_bf, adversary, counts):
        x_rows, col_rows, label_rows, group_rows, mult_rows = row_data
        logits = total_logits(x_rows, col_rows, weights_bf)
        label_hot = (label_rows[:, None] == class_range[None, :]).astype(jnp.float32)
        group_hot = (group_rows[:, None] == group_range[None, :]).astype(jnp.float32)
        log_total = jax.nn.logsumexp(logits, axis=-1)
        cross = log_total - jnp.sum(logits * label_hot, axis=-1)
        probs = jnp.exp(logits - log_total[:, None])
        local_loss = jnp.dot(mult_rows * cross, group_hot, precision=lax.Precision.HIGHEST)
        loss = lax.psum(local_loss, "samp") / counts
        coef = jnp.dot(group_hot, adversary / counts, precision=lax.Precision.HIGHEST) * mult_rows
        dz_rows = (coef[:, None] * (probs - label_hot)).astype(jnp.bfloat16)
        blocks_here = x_rows.shape[0]
        dz_blocks = dz_rows.reshape(blocks_here, block_size, classes)
        grad_tiles = jnp.einsum(
            "rbij,ric->rbjc", x_rows, dz_blocks, preferred_element_type=jnp.float32
        )
        grad_tiles = grad_tiles.reshape(blocks_here * per_row, block_size * classes)
        col_hot = (col_rows.reshape(-1)[:, None] == col_range[None, :]).astype(jnp.float32)
        grad_local = jnp.dot(col_hot.T, grad_tiles, precision=lax.Precision.HIGHEST)
        return (loss, grad_local.reshape(feat_rows, classes))

    def advance(state, grad_local):
        grad_total = lax.psum(grad_local, "samp")
        new_state = state - step_rate * grad_total
        return (new_state, new_state.astype(jnp.bfloat16))

    state = w_init
    weights_bf = w_init.astype(jnp.bfloat16)
    adversary = jnp.full((GRP,), 1.0 / GRP, jnp.float32)
    for step in range(STEPS):
        block_hits = jnp.sum(
            (picks[step][:, None] == block_range[None, :]).astype(jnp.float32), axis=0
        )
        counts = jnp.dot(block_hits, block_groups, precision=lax.Precision.HIGHEST)
        own_hits = lax.dynamic_slice_in_dim(block_hits, own_start, row_blocks, 0)
        row_data = (x_blocks, own_cols, own_labels, own_groups, jnp.repeat(own_hits, block_size))
        loss_first, grad_first = evaluate(row_data, weights_bf, adversary, counts)
        half_state, half_bf = advance(state, grad_first)
        half_adv = jax.nn.softmax(jnp.log(adversary) + adv_rate * loss_first)
        loss_second, grad_second = evaluate(row_data, half_bf, half_adv, counts)
        state, weights_bf = advance(state, grad_second)
        adversary = jax.nn.softmax(jnp.log(adversary) + adv_rate * loss_second)
    return (total_logits(x_blocks, own_cols, weights_bf), adversary)


def solution(mesh):
    in_specs = (
        P(("groups", "samp"), "feat", None, None),
        P("groups", "feat"),
        P("groups"),
        P("groups"),
        P(None, "groups"),
        P("feat", None),
    )
    out_specs = (P(("groups", "samp"), None), P("groups"))
    return jax.shard_map(
        per_device, mesh=mesh, in_specs=in_specs, out_specs=out_specs, check_vma=False
    )
```

profile of v0, /device:TPU:0, one launch (start us, length us, event | category | flops | bytes accessed | tf_op | source)
XLA Modules:
  0.0 842.0 jit_solution(14522523979013200713)
XLA Ops:
  16.2 33.7 %all-reduce.17.cloned.1.call-done = f32[8,128,64]{1,2,0:T(8,128)} async-done(((f32[8,128,64]{1,2,0:T(8,128)}), f32[8,128,64]{1,2,0:T(8,128)}) %all-reduce.17.cloned.1.call-update) | async-done | bytes 262160 | tf_op jit(solution)/shard_map/psum | solution.py:40
  56.8 6.9 copy.85
  63.7 7.9 reshape.440
  80.9 51.9 %all-reduce.19.cloned.1.call-done = f32[4096,64]{0,1:T(8,128)} async-done(((f32[4096,64]{0,1:T(8,128)}), f32[4096,64]{0,1:T(8,128)}) %all-reduce.19.cloned.1.call-update) | async-done | bytes 1048592 | tf_op jit(solution)/shard_map/psum | solution.py:66
  136.4 5.1 convolution_bitcast_fusion.11
  141.5 31.5 %all-reduce.21.cloned.1.call-done = f32[8,128,64]{1,2,0:T(8,128)} async-done(((f32[8,128,64]{1,2,0:T(8,128)}), f32[8,128,64]{1,2,0:T(8,128)}) %all-reduce.21.cloned.1.call-update) | async-done | bytes 262160 | tf_op jit(solution)/shard_map/psum | solution.py:40
  175.8 12.2 %all-reduce.2 = (f32[8]{0:T(128)S(1)}, f32[8]{0:T(128)S(1)}) all-reduce(f32[8]{0:T(128)S(1)} %convolution_bitcast_fusion.21, f32[8]{0:T(128)S(1)} %convolution_bitcast_fusion.20), channel_id=1, replica_groups=mesh['groups'=2,'samp'=4,'feat'=4] {'samp'}, use_global_device_ids=true, to_apply=%region_5.0 | all-reduce | flops 16 | bytes 128 | tf_op jit(solution)/shard_map/psum | solution.py:52
  197.3 6.9 copy.88
  204.2 7.9 reshape.443
  223.3 47.3 %all-reduce.23.cloned.1.call-done = f32[4096,64]{0,1:T(8,128)} async-done(((f32[4096,64]{0,1:T(8,128)}), f32[4096,64]{0,1:T(8,128)}) %all-reduce.23.cloned.1.call-update) | async-done | bytes 1048592 | tf_op jit(solution)/shard_map/psum | solution.py:66
  274.1 5.1 convolution_bitcast_fusion.10
  279.3 31.4 %all-reduce.25.cloned.1.call-done = f32[8,128,64]{1,2,0:T(8,128)} async-done(((f32[8,128,64]{1,2,0:T(8,128)}), f32[8,128,64]{1,2,0:T(8,128)}) %all-reduce.25.cloned.1.call-update) | async-done | bytes 262160 | tf_op jit(solution)/shard_map/psum | solution.py:40
  317.7 6.9 copy.91
  324.6 7.9 reshape.447
  344.0 51.8 %all-reduce.27.cloned.1.call-done = f32[4096,64]{0,1:T(8,128)} async-done(((f32[4096,64]{0,1:T(8,128)}), f32[4096,64]{0,1:T(8,128)}) %all-reduce.27.cloned.1.call-update) | async-done | bytes 1048592 | tf_op jit(solution)/shard_map/psum | solution.py:66
  399.3 5.1 convolution_bitcast_fusion.9
  404.4 31.4 %all-reduce.29.cloned.1.call-done = f32[8,128,64]{1,2,0:T(8,128)} async-done(((f32[8,128,64]{1,2,0:T(8,128)}), f32[8,128,64]{1,2,0:T(8,128)}) %all-reduce.29.cloned.1.call-update) | async-done | bytes 262160 | tf_op jit(solution)/shard_map/psum | solution.py:40
  438.7 11.7 %all-reduce.1 = (f32[8]{0:T(128)S(1)}, f32[8]{0:T(128)S(1)}) all-reduce(f32[8]{0:T(128)S(1)} %convolution_bitcast_fusion.19, f32[8]{0:T(128)S(1)} %convolution_bitcast_fusion.18), channel_id=1, replica_groups=mesh['groups'=2,'samp'=4,'feat'=4] {'samp'}, use_global_device_ids=true, to_apply=%region_23.0 | all-reduce | flops 16 | bytes 128 | tf_op jit(solution)/shard_map/psum | solution.py:52
  455.9 5.0 convolution_bitcast_fusion.2
  460.9 6.9 copy.94
  467.8 7.9 reshape.450
  490.0 46.1 %all-reduce.31.cloned.1.call-done = f32[4096,64]{0,1:T(8,128)} async-done(((f32[4096,64]{0,1:T(8,128)}), f32[4096,64]{0,1:T(8,128)}) %all-reduce.31.cloned.1.call-update) | async-done | bytes 1048592 | tf_op jit(solution)/shard_map/psum | solution.py:66
  544.4 31.2 %all-reduce.33.cloned.1.call-done = f32[8,128,64]{1,2,0:T(8,128)} async-done(((f32[8,128,64]{1,2,0:T(8,128)}), f32[8,128,64]{1,2,0:T(8,128)}) %all-reduce.33.cloned.1.call-update) | async-done | bytes 262160 | tf_op jit(solution)/shard_map/psum | solution.py:40
  582.7 6.9 copy.97
  589.6 7.9 reshape.454
  606.7 51.9 %all-reduce.35.cloned.1.call-done = f32[4096,64]{0,1:T(8,128)} async-done(((f32[4096,64]{0,1:T(8,128)}), f32[4096,64]{0,1:T(8,128)}) %all-reduce.35.cloned.1.call-update) | async-done | bytes 1048592 | tf_op jit(solution)/shard_map/psum | solution.py:66
  665.5 31.5 %all-reduce.37.cloned.1.call-done = f32[8,128,64]{1,2,0:T(8,128)} async-done(((f32[8,128,64]{1,2,0:T(8,128)}), f32[8,128,64]{1,2,0:T(8,128)}) %all-reduce.37.cloned.1.call-update) | async-done | bytes 262160 | tf_op jit(solution)/shard_map/psum | solution.py:40
  699.8 11.7 %all-reduce = (f32[8]{0:T(128)S(1)}, f32[8]{0:T(128)S(1)}) all-reduce(f32[8]{0:T(128)S(1)} %convolution_bitcast_fusion.17, f32[8]{0:T(128)S(1)} %convolution_bitcast_fusion.16), channel_id=1, replica_groups=mesh['groups'=2,'samp'=4,'feat'=4] {'samp'}, use_global_device_ids=true, to_apply=%region_40.0 | all-reduce | flops 16 | bytes 128 | tf_op jit(solution)/shard_map/psum | solution.py:52
  722.0 6.9 copy.100
  728.9 7.9 reshape.457
  747.3 47.9 %all-reduce.39.cloned.1.call-done = f32[4096,64]{0,1:T(8,128)} async-done(((f32[4096,64]{0,1:T(8,128)}), f32[4096,64]{0,1:T(8,128)}) %all-reduce.39.cloned.1.call-update) | async-done | bytes 1048592 | tf_op jit(solution)/shard_map/psum | solution.py:66
  803.8 29.7 %all-reduce.41.cloned.1.call-done = f32[1024,64]{0,1:T(8,128)} async-done(((f32[1024,64]{0,1:T(8,128)}), f32[1024,64]{0,1:T(8,128)}) %all-reduce.41.cloned.1.call-update) | async-done | bytes 262160 | tf_op jit(solution)/shard_map/psum | solution.py:40
  (161 shorter events, 165.7 us)
Async XLA Ops:
  7.2 9.0 %copy-start = (s32[4096]{0:T(1024)S(1)}, s32[4096]{0:T(1024)}, u32[]{:S(2)}) copy-start(s32[4096]{0:T(1024)} %param.8) | copy-start | bytes 49156
  7.2 42.6 %all-reduce.17.cloned.1.call-start = ((), (), s32[]{:S(2)}) async-start(), calls=%async_computation | async-start | bytes 524288 | tf_op jit(solution)/shard_map/psum | solution.py:40
  10.5 4.5 copy-start.7
  10.5 4.7 copy-start.6
  15.0 117.8 %all-reduce.19.cloned.1.call-start = ((), (), s32[]{:S(2)}) async-start(), calls=%async_computation.1 | async-start | bytes 2097152 | tf_op jit(solution)/shard_map/psum | solution.py:66
  75.4 57.4 %copy-start.2 = (f32[4096,64]{0,1:T(8,128)S(1)}, f32[4096,64]{0,1:T(8,128)}, u32[]{:S(2)}) copy-start(f32[4096,64]{0,1:T(8,128)} %param.11) | copy-start | bytes 3145732
  80.8 92.1 %all-reduce.21.cloned.1.call-start = ((), (), s32[]{:S(2)}) async-start(), calls=%async_computation.2 | async-start | bytes 524288 | tf_op jit(solution)/shard_map/psum | solution.py:40
  141.4 129.2 %all-reduce.23.cloned.1.call-start = ((), (), s32[]{:S(2)}) async-start(), calls=%async_computation.3 | async-start | bytes 2097152 | tf_op jit(solution)/shard_map/psum | solution.py:66
  221.3 89.4 %all-reduce.25.cloned.1.call-start = ((), (), s32[]{:S(2)}) async-start(), calls=%async_computation.4 | async-start | bytes 524288 | tf_op jit(solution)/shard_map/psum | solution.py:40
  279.2 116.5 %all-reduce.27.cloned.1.call-start = ((), (), s32[]{:S(2)}) async-start(), calls=%async_computation.5 | async-start | bytes 2097152 | tf_op jit(solution)/shard_map/psum | solution.py:66
  337.3 58.4 %copy-start.3 = (f32[4096,64]{0,1:T(8,128)S(1)}, f32[4096,64]{0,1:T(8,128)}, u32[]{:S(2)}) copy-start(f32[4096,64]{0,1:T(8,128)} %all-reduce.23.cloned.1.call-done) | copy-start | bytes 3145732
  343.7 92.1 %all-reduce.29.cloned.1.call-start = ((), (), s32[]{:S(2)}) async-start(), calls=%async_computation.6 | async-start | bytes 524288 | tf_op jit(solution)/shard_map/psum | solution.py:40
  404.4 131.7 %all-reduce.31.cloned.1.call-start = ((), (), s32[]{:S(2)}) async-start(), calls=%async_computation.7 | async-start | bytes 2097152 | tf_op jit(solution)/shard_map/psum | solution.py:66
  486.8 88.9 %all-reduce.33.cloned.1.call-start = ((), (), s32[]{:S(2)}) async-start(), calls=%async_computation.8 | async-start | bytes 524288 | tf_op jit(solution)/shard_map/psum | solution.py:40
  544.1 114.6 %all-reduce.35.cloned.1.call-start = ((), (), s32[]{:S(2)}) async-start(), calls=%async_computation.9 | async-start | bytes 2097152 | tf_op jit(solution)/shard_map/psum | solution.py:66
  601.3 57.4 %copy-start.4 = (f32[4096,64]{0,1:T(8,128)S(1)}, f32[4096,64]{0,1:T(8,128)}, u32[]{:S(2)}) copy-start(f32[4096,64]{0,1:T(8,128)} %get-tuple-element.29) | copy-start | bytes 3145732
  606.7 90.3 %all-reduce.37.cloned.1.call-start = ((), (), s32[]{:S(2)}) async-start(), calls=%async_computation.10 | async-start | bytes 524288 | tf_op jit(solution)/shard_map/psum | solution.py:40
  665.4 129.8 %all-reduce.39.cloned.1.call-start = ((), (), s32[]{:S(2)}) async-start(), calls=%async_computation.11 | async-start | bytes 2097152 | tf_op jit(solution)/shard_map/psum | solution.py:66
  740.6 54.6 %copy-start.5 = (f32[4096,64]{0,1:T(8,128)S(1)}, f32[4096,64]{0,1:T(8,128)}, u32[]{:S(2)}) copy-start(f32[4096,64]{0,1:T(8,128)} %get-tuple-element.29) | copy-start | bytes 3145732
  746.0 87.6 %all-reduce.41.cloned.1.call-start = ((), (), s32[]{:S(2)}) async-start(), calls=%async_computation.12 | async-start | bytes 524288 | tf_op jit(solution)/shard_map/psum | solution.py:40
  796.6 38.6 %copy-start.1 = (s32[4096]{0:T(1024)S(1)}, s32[4096]{0:T(1024)}, u32[]{:S(2)}) copy-start(s32[4096]{0:T(1024)} %param.8) | copy-start | bytes 49156
Sparse Core Ops, SparseCore 0:
  15.1 34.6 all-reduce.16
  80.9 51.8 all-reduce.18
  141.6 31.3 all-reduce.20
  221.4 49.1 all-reduce.22
  279.3 31.3 all-reduce.24
  343.9 51.8 all-reduce.26
  404.5 31.3 all-reduce.28
  486.9 49.1 all-reduce.30
  544.2 31.4 all-reduce.32
  606.8 51.8 all-reduce.34
  665.5 31.3 all-reduce.36
  746.1 49.0 all-reduce.38
  802.2 31.3 all-reduce.40
where the time goes:
time: 851 us; the launch traced here: 842 us
  waiting for transfers between devices  518 us (61%)
  local copies, waits for them, and re-layouts  136 us (16%)
  matrix products  98.5 us (12%)
  other arithmetic  38.8 us (5%)
  blocking collectives  35.5 us (4%)
  between operations  14.6 us (2%)
    psum x6, waiting for transfers between devices, advance(): grad_total = lax.psum(grad_local, 'samp')  297 us
    psum x7, waiting for transfers between devices, total_logits(): summed = lax.psum(partial_sum, 'feat')  220 us
    reshape x6, local copies, waits for them, and re-layouts, evaluate(): grad_tiles = grad_tiles.reshape(blocks_here * per_row, block_size * classes)  47.3 us
    dot_general x6, local copies, waits for them, and re-layouts, evaluate(): jnp.einsum('rbij,ric->rbjc', x_rows, dz_blocks, preferred_element_type=jn...  41.4 us
    psum x3, blocking collectives, evaluate(): loss = lax.psum(local_loss, 'samp') / counts  35.5 us
    reshape x12, local copies, waits for them, and re-layouts, evaluate(): return (loss, grad_local.reshape(feat_rows, classes))  34.1 us
    dot_general x7, matrix products, total_logits(): jnp.einsum('rbij,rbjc->ric', x_rows, tiles, preferred_element_type=jnp.fl...  32.2 us
    dot_general x6, matrix products, evaluate(): jnp.einsum('rbij,ric->rbjc', x_rows, dz_blocks, preferred_element_type=jn...  29.8 us
  transfers between devices with their start and end apart: 13, of which 13 were waited for; matrix products, arithmetic and copies ran while one was open for 1% of the time, Pallas kernels for 0%

commit v1 on v0

--- a/solution.py
+++ b/solution.py
@@ -37,7 +37,8 @@
         partial_sum = jnp.einsum(
             "rbij,rbjc->ric", x_rows, tiles, preferred_element_type=jnp.float32
         )
-        summed = lax.psum(partial_sum, "feat")
+        blocks = lax.all_gather(partial_sum, "feat", axis=0, tiled=False)
+        summed = blocks.sum(axis=0)
         return summed.reshape(-1, classes)
 
     def evaluate(row_data, weights_bf, adversary, counts):

time: 851 us -> 741 us (0.87)
  waiting for transfers between devices: 518 us -> 410 us
    psum x7 -> x0, waiting for transfers between devices: 220 us -> none  [total_logits(): summed = lax.psum(partial_sum, 'feat')]
    all_gather x0 -> x7, waiting for transfers between devices: none -> 107 us  [total_logits(): blocks = lax.all_gather(partial_sum, 'feat', axis=0, tiled=False)]
    reduce_sum x0 -> x7, other arithmetic: none -> 9.16 us  [total_logits(): summed = blocks.sum(axis=0)]
where the time goes in v1:
time: 741 us; the launch traced here: 732 us
  waiting for transfers between devices  410 us (55%)
  local copies, waits for them, and re-layouts  135 us (18%)
  matrix products  98.8 us (13%)
  other arithmetic  36.5 us (5%)
  blocking collectives  35.9 us (5%)
  between operations  14.7 us (2%)
    psum x6, waiting for transfers between devices, advance(): grad_total = lax.psum(grad_local, 'samp')  303 us
    all_gather x7, waiting for transfers between devices, total_logits(): blocks = lax.all_gather(partial_sum, 'feat', axis=0, tiled=False)  107 us
    reshape x6, local copies, waits for them, and re-layouts, evaluate(): grad_tiles = grad_tiles.reshape(blocks_here * per_row, block_size * classes)  47.3 us
    dot_general x6, local copies, waits for them, and re-layouts, evaluate(): jnp.einsum('rbij,ric->rbjc', x_rows, dz_blocks, preferred_element_type=jn...  41.4 us
    psum x3, blocking collectives, evaluate(): loss = lax.psum(local_loss, 'samp') / counts  35.9 us
    reshape x12, local copies, waits for them, and re-layouts, evaluate(): return (loss, grad_local.reshape(feat_rows, classes))  34.1 us
    dot_general x7, matrix products, total_logits(): jnp.einsum('rbij,rbjc->ric', x_rows, tiles, preferred_element_type=jnp.fl...  32.9 us
    dot_general x6, matrix products, evaluate(): jnp.einsum('rbij,ric->rbjc', x_rows, dz_blocks, preferred_element_type=jn...  29.2 us
  transfers between devices with their start and end apart: 13, of which 13 were waited for; matrix products, arithmetic and copies ran while one was open for 1% of the time, Pallas kernels for 0%

profile of v1, /device:TPU:0, one launch (start us, length us, event | category | flops | bytes accessed | tf_op | source)
XLA Modules:
  0.0 731.8 jit_solution(494705189807476659)
XLA Ops:
  16.2 18.4 %all-gather.15.cloned.1.call-done = f32[32,128,64]{1,2,0:T(8,128)} async-done(((f32[8,128,64]{1,2,0:T(8,128)}), f32[32,128,64]{1,2,0:T(8,128)}) %all-gather.15.cloned.1.call-update) | async-done | bytes 1048592 | tf_op jit(solution)/shard_map/all_gather | solution.py:40
  40.9 6.9 copy.130
  47.8 7.9 %reshape.440 = f32[128,8192]{1,0:T(8,128)} reshape(f32[8,16,128,64]{3,2,1,0:T(8,128)} %copy.130) | data formatting | bytes 8388608 | tf_op jit(solution)/shard_map/reshape | solution.py:61
  64.9 51.9 %all-reduce.10.cloned.1.call-done = f32[4096,64]{0,1:T(8,128)} async-done(((f32[4096,64]{0,1:T(8,128)}), f32[4096,64]{0,1:T(8,128)}) %all-reduce.10.cloned.1.call-update) | async-done | bytes 1048592 | tf_op jit(solution)/shard_map/psum | solution.py:67
  120.4 5.1 convolution_bitcast_fusion.11
  125.6 16.2 %all-gather.17.cloned.1.call-done = f32[32,128,64]{1,2,0:T(8,128)} async-done(((f32[8,128,64]{1,2,0:T(8,128)}), f32[32,128,64]{1,2,0:T(8,128)}) %all-gather.17.cloned.1.call-update) | async-done | bytes 1048592 | tf_op jit(solution)/shard_map/all_gather | solution.py:40
  144.1 12.2 %all-reduce.2 = (f32[8]{0:T(128)S(1)}, f32[8]{0:T(128)S(1)}) all-reduce(f32[8]{0:T(128)S(1)} %convolution_bitcast_fusion.21, f32[8]{0:T(128)S(1)} %convolution_bitcast_fusion.20), channel_id=1, replica_groups=mesh['groups'=2,'samp'=4,'feat'=4] {'samp'}, use_global_device_ids=true, to_apply=%region_5.0 | all-reduce | flops 16 | bytes 128 | tf_op jit(solution)/shard_map/psum | solution.py:53
  165.6 6.9 copy.133
  172.5 7.9 %reshape.443 = f32[128,8192]{1,0:T(8,128)} reshape(f32[8,16,128,64]{3,2,1,0:T(8,128)} %copy.133) | data formatting | bytes 8388608 | tf_op jit(solution)/shard_map/reshape | solution.py:61
  189.6 49.2 %all-reduce.12.cloned.1.call-done = f32[4096,64]{0,1:T(8,128)} async-done(((f32[4096,64]{0,1:T(8,128)}), f32[4096,64]{0,1:T(8,128)}) %all-reduce.12.cloned.1.call-update) | async-done | bytes 1048592 | tf_op jit(solution)/shard_map/psum | solution.py:67
  242.4 5.1 convolution_bitcast_fusion.10
  249.6 14.2 %all-gather.19.cloned.1.call-done = f32[32,128,64]{1,2,0:T(8,128)} async-done(((f32[8,128,64]{1,2,0:T(8,128)}), f32[32,128,64]{1,2,0:T(8,128)}) %all-gather.19.cloned.1.call-update) | async-done | bytes 1048592 | tf_op jit(solution)/shard_map/all_gather | solution.py:40
  270.0 6.9 copy.136
  276.9 7.9 %reshape.447 = f32[128,8192]{1,0:T(8,128)} reshape(f32[8,16,128,64]{3,2,1,0:T(8,128)} %copy.136) | data formatting | bytes 8388608 | tf_op jit(solution)/shard_map/reshape | solution.py:61
  296.3 51.8 %all-reduce.14.cloned.1.call-done = f32[4096,64]{0,1:T(8,128)} async-done(((f32[4096,64]{0,1:T(8,128)}), f32[4096,64]{0,1:T(8,128)}) %all-reduce.14.cloned.1.call-update) | async-done | bytes 1048592 | tf_op jit(solution)/shard_map/psum | solution.py:67
  351.6 5.1 convolution_bitcast_fusion.9
  356.7 16.2 %all-gather.21.cloned.1.call-done = f32[32,128,64]{1,2,0:T(8,128)} async-done(((f32[8,128,64]{1,2,0:T(8,128)}), f32[32,128,64]{1,2,0:T(8,128)}) %all-gather.21.cloned.1.call-update) | async-done | bytes 1048592 | tf_op jit(solution)/shard_map/all_gather | solution.py:40
  375.2 11.7 %all-reduce.1 = (f32[8]{0:T(128)S(1)}, f32[8]{0:T(128)S(1)}) all-reduce(f32[8]{0:T(128)S(1)} %convolution_bitcast_fusion.19, f32[8]{0:T(128)S(1)} %convolution_bitcast_fusion.18), channel_id=1, replica_groups=mesh['groups'=2,'samp'=4,'feat'=4] {'samp'}, use_global_device_ids=true, to_apply=%region_23.0 | all-reduce | flops 16 | bytes 128 | tf_op jit(solution)/shard_map/psum | solution.py:53
  397.3 6.9 copy.139
  404.2 7.9 %reshape.450 = f32[128,8192]{1,0:T(8,128)} reshape(f32[8,16,128,64]{3,2,1,0:T(8,128)} %copy.139) | data formatting | bytes 8388608 | tf_op jit(solution)/shard_map/reshape | solution.py:61
  423.2 49.2 %all-reduce.16.cloned.1.call-done = f32[4096,64]{0,1:T(8,128)} async-done(((f32[4096,64]{0,1:T(8,128)}), f32[4096,64]{0,1:T(8,128)}) %all-reduce.16.cloned.1.call-update) | async-done | bytes 1048592 | tf_op jit(solution)/shard_map/psum | solution.py:67
  483.9 12.8 %all-gather.23.cloned.1.call-done = f32[32,128,64]{1,2,0:T(8,128)} async-done(((f32[8,128,64]{1,2,0:T(8,128)}), f32[32,128,64]{1,2,0:T(8,128)}) %all-gather.23.cloned.1.call-update) | async-done | bytes 1048592 | tf_op jit(solution)/shard_map/all_gather | solution.py:40
  503.0 6.9 copy.142
  509.9 7.9 %reshape.454 = f32[128,8192]{1,0:T(8,128)} reshape(f32[8,16,128,64]{3,2,1,0:T(8,128)} %copy.142) | data formatting | bytes 8388608 | tf_op jit(solution)/shard_map/reshape | solution.py:61
  527.1 51.9 %all-reduce.18.cloned.1.call-done = f32[4096,64]{0,1:T(8,128)} async-done(((f32[4096,64]{0,1:T(8,128)}), f32[4096,64]{0,1:T(8,128)}) %all-reduce.18.cloned.1.call-update) | async-done | bytes 1048592 | tf_op jit(solution)/shard_map/psum | solution.py:67
  585.8 16.2 %all-gather.25.cloned.1.call-done = f32[32,128,64]{1,2,0:T(8,128)} async-done(((f32[8,128,64]{1,2,0:T(8,128)}), f32[32,128,64]{1,2,0:T(8,128)}) %all-gather.25.cloned.1.call-update) | async-done | bytes 1048592 | tf_op jit(solution)/shard_map/all_gather | solution.py:40
  604.4 11.9 %all-reduce = (f32[8]{0:T(128)S(1)}, f32[8]{0:T(128)S(1)}) all-reduce(f32[8]{0:T(128)S(1)} %convolution_bitcast_fusion.17, f32[8]{0:T(128)S(1)} %convolution_bitcast_fusion.16), channel_id=1, replica_groups=mesh['groups'=2,'samp'=4,'feat'=4] {'samp'}, use_global_device_ids=true, to_apply=%region_40.0 | all-reduce | flops 16 | bytes 128 | tf_op jit(solution)/shard_map/psum | solution.py:53
  621.8 4.9 convolution_bitcast_fusion
  626.7 6.9 copy.145
  633.6 7.9 %reshape.457 = f32[128,8192]{1,0:T(8,128)} reshape(f32[8,16,128,64]{3,2,1,0:T(8,128)} %copy.145) | data formatting | bytes 8388608 | tf_op jit(solution)/shard_map/reshape | solution.py:61
  650.7 49.2 %all-reduce.20.cloned.1.call-done = f32[4096,64]{0,1:T(8,128)} async-done(((f32[4096,64]{0,1:T(8,128)}), f32[4096,64]{0,1:T(8,128)}) %all-reduce.20.cloned.1.call-update) | async-done | bytes 1048592 | tf_op jit(solution)/shard_map/psum | solution.py:67
  709.8 13.2 %all-gather.27.cloned.1.call-done = f32[32,128,64]{1,2,0:T(8,128)} async-done(((f32[8,128,64]{1,2,0:T(8,128)}), f32[32,128,64]{1,2,0:T(8,128)}) %all-gather.27.cloned.1.call-update) | async-done | bytes 1048592 | tf_op jit(solution)/shard_map/all_gather | solution.py:40
  (167 shorter events, 162.2 us)
Async XLA Ops:
  7.2 8.2 %copy-start = (s32[4096]{0:T(1024)S(1)}, s32[4096]{0:T(1024)}, u32[]{:S(2)}) copy-start(s32[4096]{0:T(1024)} %param.8) | copy-start | bytes 49156
  7.2 27.4 %all-gather.15.cloned.1.call-start = ((), (), s32[]{:S(2)}) async-start(), calls=%async_computation.6 | async-start | bytes 1310720 | tf_op jit(solution)/shard_map/all_gather | solution.py:40
  10.5 4.5 copy-start.7
  10.5 4.9 copy-start.6
  15.0 101.9 %all-reduce.10.cloned.1.call-start = ((), (), s32[]{:S(2)}) async-start(), calls=%async_computation | async-start | bytes 2097152 | tf_op jit(solution)/shard_map/psum | solution.py:67
  59.5 57.4 %copy-start.2 = (f32[4096,64]{0,1:T(8,128)S(1)}, f32[4096,64]{0,1:T(8,128)}, u32[]{:S(2)}) copy-start(f32[4096,64]{0,1:T(8,128)} %param.11) | copy-start | bytes 3145732
  64.9 76.9 %all-gather.17.cloned.1.call-start = ((), (), s32[]{:S(2)}) async-start(), calls=%async_computation.7 | async-start | bytes 1310720 | tf_op jit(solution)/shard_map/all_gather | solution.py:40
  125.5 113.3 %all-reduce.12.cloned.1.call-start = ((), (), s32[]{:S(2)}) async-start(), calls=%async_computation.1 | async-start | bytes 2097152 | tf_op jit(solution)/shard_map/psum | solution.py:67
  189.6 74.1 %all-gather.19.cloned.1.call-start = ((), (), s32[]{:S(2)}) async-start(), calls=%async_computation.8 | async-start | bytes 1310720 | tf_op jit(solution)/shard_map/all_gather | solution.py:40
  247.4 100.6 %all-reduce.14.cloned.1.call-start = ((), (), s32[]{:S(2)}) async-start(), calls=%async_computation.2 | async-start | bytes 2097152 | tf_op jit(solution)/shard_map/psum | solution.py:67
  289.6 58.4 %copy-start.3 = (f32[4096,64]{0,1:T(8,128)S(1)}, f32[4096,64]{0,1:T(8,128)}, u32[]{:S(2)}) copy-start(f32[4096,64]{0,1:T(8,128)} %all-reduce.12.cloned.1.call-done) | copy-start | bytes 3145732
  296.0 76.9 %all-gather.21.cloned.1.call-start = ((), (), s32[]{:S(2)}) async-start(), calls=%async_computation.9 | async-start | bytes 1310720 | tf_op jit(solution)/shard_map/all_gather | solution.py:40
  356.7 115.7 %all-reduce.16.cloned.1.call-start = ((), (), s32[]{:S(2)}) async-start(), calls=%async_computation.3 | async-start | bytes 2097152 | tf_op jit(solution)/shard_map/psum | solution.py:67
  423.2 73.5 %all-gather.23.cloned.1.call-start = ((), (), s32[]{:S(2)}) async-start(), calls=%async_computation.10 | async-start | bytes 1310720 | tf_op jit(solution)/shard_map/all_gather | solution.py:40
  480.4 98.6 %all-reduce.18.cloned.1.call-start = ((), (), s32[]{:S(2)}) async-start(), calls=%async_computation.4 | async-start | bytes 2097152 | tf_op jit(solution)/shard_map/psum | solution.py:67
  521.6 57.4 %copy-start.4 = (f32[4096,64]{0,1:T(8,128)S(1)}, f32[4096,64]{0,1:T(8,128)}, u32[]{:S(2)}) copy-start(f32[4096,64]{0,1:T(8,128)} %get-tuple-element.29) | copy-start | bytes 3145732
  527.0 75.0 %all-gather.25.cloned.1.call-start = ((), (), s32[]{:S(2)}) async-start(), calls=%async_computation.11 | async-start | bytes 1310720 | tf_op jit(solution)/shard_map/all_gather | solution.py:40
  585.8 114.1 %all-reduce.20.cloned.1.call-start = ((), (), s32[]{:S(2)}) async-start(), calls=%async_computation.5 | async-start | bytes 2097152 | tf_op jit(solution)/shard_map/psum | solution.py:67
  645.3 54.6 %copy-start.5 = (f32[4096,64]{0,1:T(8,128)S(1)}, f32[4096,64]{0,1:T(8,128)}, u32[]{:S(2)}) copy-start(f32[4096,64]{0,1:T(8,128)} %get-tuple-element.29) | copy-start | bytes 3145732
  650.7 72.3 %all-gather.27.cloned.1.call-start = ((), (), s32[]{:S(2)}) async-start(), calls=%async_computation.12 | async-start | bytes 1310720 | tf_op jit(solution)/shard_map/all_gather | solution.py:40
  702.3 22.8 %copy-start.1 = (s32[4096]{0:T(1024)S(1)}, s32[4096]{0:T(1024)}, u32[]{:S(2)}) copy-start(s32[4096]{0:T(1024)} %param.8) | copy-start | bytes 49156
Sparse Core Ops, SparseCore 0:
  15.1 19.4 all-gather.14
  65.0 51.8 all-reduce.9
  125.6 16.0 all-gather.16
  189.7 49.0 all-reduce.11
  247.6 16.0 all-gather.18
  296.1 51.8 all-reduce.13
  356.8 16.1 all-gather.20
  423.3 49.0 all-reduce.15
  480.6 16.0 all-gather.22
  527.1 51.8 all-reduce.17
  585.9 16.1 all-gather.24
  650.8 49.0 all-reduce.19
  706.8 16.0 all-gather.26
